TPU v7x, 32 devices: a whole 2x2x4 slice. The times are simulated.
32 devices in a mesh: row: 4 (over y, x), col: 8 (over z, core).
Axes of the slice: x: 2, y: 2, z: 4, core: 2. Of those that a mesh axis runs over, the one named last changes fastest.
Arguments:
- rhs: float32 [4, 8, 4608], P('row', 'col'), may hold values from -14 to 14
- friction: float32 [4, 8, 4608], P('row', 'col'), may hold values from 1 to 4
- kernel_tiles: bfloat16 [4, 8, 256, 128, 128], P('row', 'col'), may hold values from -0.1875 to 0.1875
- tile_scale: float32 [4, 8, 256], P('row', 'col'), may hold values from 0.5 to 2
- tile_row: int32 [4, 8, 256], P('row', 'col'), may hold values from 0 to 287, as said below
- tile_col: int32 [4, 8, 256], P('row', 'col'), may hold values from 0 to 143
- tile_counts: int32 [4, 8], P('row', 'col'), may hold values from 64 to 256, as said below
- precond_blocks: bfloat16 [4, 8, 24, 512, 512], P('row', 'col'), may hold values from -3 to 3, as said below
- fault_sizes: int32 [4, 8, 24], P('row', 'col'), may hold values from 1 to 512, 4608 in all within a row
Outputs:
- update: float32 [4, 8, 4608], P('row', 'col')
- residual: float32 [4, 8, 4608], P('row', 'col')
Inputs may be any that keep to these rules, and one draw needn't show every extreme that they name: Row tile within the row group; in every block (r, c), over all 256 slots, at most 64 slots have the same tile_row // 36, and some value of it has exactly 64. `tile_counts`: slots at or beyond the count hold no kernel tile and are ignored; some block has 256 live slots and some 256 // 4. `fault_sizes`: the faults of each (r, c) cover its 4608 elements in order; each (r, c) has a fault of exactly 512 elements. `precond_blocks`: entries of a block outside its fault's size are ignored.
All inputs are finite; a program needn't handle non-finite values.
Results may differ from a plain program's by a relative error of at most 0.012.
Values may be sent and summed in bfloat16 or wider, within the bound.
No kernel may reach another device: no remote copies, remote signals or barrier semaphores. Data moves between devices by JAX's collectives and lax.ppermute only.
A program may use at most 64 MiB of HBM per device.

v0:
```python
import jax
import jax.numpy as jnp
from jax import lax
from jax.sharding import PartitionSpec as P

ITERS = 3
exact_mode = lax.Precision.HIGHEST


def local(
    rhs,
    friction,
    kernel_tiles,
    tile_scale,
    tile_row,
    tile_col,
    tile_counts,
    precond_blocks,
    fault_sizes,
):
    vector_len = rhs.shape[2]
    tile_width = kernel_tiles.shape[3]
    slot_count = kernel_tiles.shape[2]
    fault_width = precond_blocks.shape[3]
    col_devices = lax.axis_size("col")
    row_tiles = col_devices * vector_len // tile_width
    local_tiles = kernel_tiles[0, 0]
    tile_rows = tile_row[0, 0]
    tile_cols = tile_col[0, 0]
    tile_weight = jnp.where(
        jnp.arange(slot_count, dtype=jnp.int32) < tile_counts[0, 0], tile_scale[0, 0], 0.0
    )
    fault_blocks = precond_blocks[0, 0]
    fault_len = fault_sizes[0, 0]
    fault_starts = jnp.cumsum(fault_len) - fault_len
    slot_place = jnp.arange(fault_width, dtype=jnp.int32)
    gather_spot = jnp.clip(fault_starts[:, None] + slot_place[None, :], 0, vector_len - 1)
    slot_live = slot_place[None, :] < fault_len[:, None]
    element_ids = jnp.arange(vector_len, dtype=jnp.int32)
    owner_fault = (
        jnp.sum((fault_starts[None, :] <= element_ids[:, None]).astype(jnp.int32), axis=1) - 1
    )
    flat_spot = owner_fault * fault_width + element_ids - fault_starts[owner_fault]

    def kernel_apply(field):
        low_field = field.astype(jnp.bfloat16).reshape(1, 1, vector_len)
        column = lax.all_gather(low_field, "row", axis=0, tiled=True)
        column_pieces = column.reshape(-1, tile_width)[tile_cols]
        products = (
            jnp.einsum("tij,tj->ti", local_tiles, column_pieces, preferred_element_type=jnp.float32)
            * tile_weight[:, None]
        )
        partial_value = jax.ops.segment_sum(products, tile_rows, num_segments=row_tiles).reshape(-1)
        row_total = lax.psum(partial_value, "col")
        return lax.dynamic_slice_in_dim(row_total, lax.axis_index("col") * vector_len, vector_len)

    rhs_flat = rhs.reshape(-1)
    friction_flat = friction.reshape(-1)

    def operator(field):
        return friction_flat * field + kernel_apply(field)

    def global_norm(field):
        return jnp.sqrt(lax.psum(jnp.sum(field * field), ("row", "col")))

    rhs_norm = global_norm(rhs_flat)
    krylov = [rhs_flat / rhs_norm]
    directions = []
    hessenberg = jnp.zeros((ITERS + 1, ITERS), jnp.float32)
    for step in range(ITERS):
        low_vector = krylov[step].astype(jnp.bfloat16)
        padded = jnp.where(slot_live, low_vector[gather_spot], jnp.zeros((), jnp.bfloat16))
        result = jnp.einsum("fij,fj->fi", fault_blocks, padded, preferred_element_type=jnp.float32)
        direction = result.reshape(-1)[flat_spot]
        directions.append(direction)
        image = operator(direction)
        height_list = []
        for earlier in krylov:
            height = lax.psum(jnp.sum(earlier * image), ("row", "col"))
            image = image - height * earlier
            height_list.append(height)
        heights = jnp.stack(height_list)
        new_norm = global_norm(image)
        hessenberg = hessenberg.at[: step + 1, step].set(heights).at[step + 1, step].set(new_norm)
        krylov.append(image / new_norm)
    gram_matrix = jnp.dot(hessenberg.T, hessenberg, precision=exact_mode)
    target = rhs_norm * hessenberg[0, :]
    lower_factor = jnp.linalg.cholesky(gram_matrix)
    weights_y = jax.scipy.linalg.cho_solve((lower_factor, True), target)
    update = jnp.dot(weights_y, jnp.stack(directions), precision=exact_mode)
    residual = rhs_flat - operator(update)
    return (update.reshape(1, 1, vector_len), residual.reshape(1, 1, vector_len))


def solution(mesh):
    return jax.shard_map(
        local,
        mesh=mesh,
        in_specs=(
            P("row", "col", None),
            P("row", "col", None),
            P("row", "col", None, None, None),
            P("row", "col", None),
            P("row", "col", None),
            P("row", "col", None),
            P("row", "col"),
            P("row", "col", None, None, None),
            P("row", "col", None),
        ),
        out_specs=(P("row", "col", None), P("row", "col", None)),
        check_vma=False,
    )
```

profile of v0, /device:TPU:8, one launch (start us, length us, event | category | flops | bytes accessed | tf_op | source)
XLA Modules:
  0.0 1087.3 jit_solution(13645294912561519744)
XLA Ops:
  10.4 4.5 fusion.50
  15.8 10.6 select_select_fusion
  27.9 40.7 %psum.98 = f32[]{:T(128)} all-reduce(f32[]{:T(128)} %multiply_reduce_fusion.9), channel_id=1, replica_groups=mesh['row'=4,'col'=8] {'row','col'}, use_global_device_ids=true, to_apply=%region_1.2 | all-reduce | flops 1 | bytes 8 | tf_op jit(solution)/shard_map/psum | solution.py:64
  69.4 75.8 %gather_fusion = bf16[12288]{0:T(1024)(128)(2,1)S(1)} fusion(bf16[4608]{0:T(1024)(128)(2,1)S(1)} %fusion.59, s32[12288]{0:T(1024)S(1)} %broadcast_clamp_fusion), kind=kCustom, calls=%fused_computation | custom fusion | bytes 98304 | tf_op jit(solution)/shard_map/gather | solution.py:72
  145.3 7.9 fusion.4
  153.3 24.1 %gather_fusion.1 = f32[4608]{0:T(1024)S(1)} fusion(f32[12288]{0:T(1024)S(1)} %bitcast.140, s32[5120]{0:T(1024)S(1)} %pad_clamp_fusion), kind=kCustom, calls=%fused_computation.1 | custom fusion | bytes 55296 | tf_op jit(solution)/shard_map/gather | solution.py:74
  177.4 9.3 all-gather.4
  188.5 7.8 fusion.12
  196.3 2.3 scatter_custom_fusion
  200.6 50.8 %all-reduce.6.cloned.1.call-done = f32[36864]{0:T(1024)} async-done(((f32[36864]{0:T(1024)}), f32[36864]{0:T(1024)}) %all-reduce.6.cloned.1.call-update) | async-done | bytes 147472 | tf_op jit(solution)/shard_map/psum | solution.py:54
  251.4 1.4 multiply_reduce_fusion.8
  252.8 39.5 %psum.100 = f32[]{:T(128)} all-reduce(f32[]{:T(128)} %get-tuple-element.99), channel_id=1, replica_groups=mesh['row'=4,'col'=8] {'row','col'}, use_global_device_ids=true, to_apply=%region_7.8 | all-reduce | flops 1 | bytes 8 | tf_op jit(solution)/shard_map/psum | solution.py:79
  293.5 40.7 %psum.101 = f32[]{:T(128)} all-reduce(f32[]{:T(128)} %multiply_reduce_fusion.7), channel_id=1, replica_groups=mesh['row'=4,'col'=8] {'row','col'}, use_global_device_ids=true, to_apply=%region_9.10 | all-reduce | flops 1 | bytes 8 | tf_op jit(solution)/shard_map/psum | solution.py:64
  335.6 75.8 %gather_fusion.3 = bf16[12288]{0:T(1024)(128)(2,1)S(1)} fusion(bf16[4608]{0:T(1024)(128)(2,1)S(1)} %fusion.60, s32[12288]{0:T(1024)S(1)} %broadcast_clamp_fusion), kind=kCustom, calls=%fused_computation.3 | custom fusion | bytes 98304 | tf_op jit(solution)/shard_map/gather | solution.py:72
  411.5 7.9 fusion.2
  419.5 24.1 %gather_fusion.4 = f32[4608]{0:T(1024)S(1)} fusion(f32[12288]{0:T(1024)S(1)} %bitcast.141, s32[5120]{0:T(1024)S(1)} %pad_clamp_fusion), kind=kCustom, calls=%fused_computation.4 | custom fusion | bytes 55296 | tf_op jit(solution)/shard_map/gather | solution.py:74
  443.6 9.3 all-gather.5
  454.0 7.8 fusion.10
  461.8 2.3 scatter_custom_fusion.1
  465.5 51.4 %all-reduce.8.cloned.1.call-done = f32[36864]{0:T(1024)} async-done(((f32[36864]{0:T(1024)}), f32[36864]{0:T(1024)}) %all-reduce.8.cloned.1.call-update) | async-done | bytes 147472 | tf_op jit(solution)/shard_map/psum | solution.py:54
  516.9 1.5 multiply_reduce_fusion.6
  518.4 39.5 %psum.103 = f32[]{:T(128)} all-reduce(f32[]{:T(128)} %get-tuple-element.97), channel_id=1, replica_groups=mesh['row'=4,'col'=8] {'row','col'}, use_global_device_ids=true, to_apply=%region_14.15 | all-reduce | flops 1 | bytes 8 | tf_op jit(solution)/shard_map/psum | solution.py:79
  557.8 2.0 multiply_reduce_fusion.5
  559.9 40.6 %psum.104 = f32[]{:T(128)} all-reduce(f32[]{:T(128)} %multiply_reduce_fusion.5), channel_id=1, replica_groups=mesh['row'=4,'col'=8] {'row','col'}, use_global_device_ids=true, to_apply=%region_16.17 | all-reduce | flops 1 | bytes 8 | tf_op jit(solution)/shard_map/psum | solution.py:79
  600.5 2.6 multiply_reduce_fusion.4
  603.2 40.5 %psum.105 = f32[]{:T(128)} all-reduce(f32[]{:T(128)} %get-tuple-element.95), channel_id=1, replica_groups=mesh['row'=4,'col'=8] {'row','col'}, use_global_device_ids=true, to_apply=%region_18.19 | all-reduce | flops 1 | bytes 8 | tf_op jit(solution)/shard_map/psum | solution.py:64
  644.4 75.8 %gather_fusion.6 = bf16[12288]{0:T(1024)(128)(2,1)S(1)} fusion(bf16[4608]{0:T(1024)(128)(2,1)S(1)} %fusion.58, s32[12288]{0:T(1024)S(1)} %broadcast_clamp_fusion), kind=kCustom, calls=%fused_computation.6 | custom fusion | bytes 98304 | tf_op jit(solution)/shard_map/gather | solution.py:72
  720.3 7.9 fusion
  728.3 24.1 %gather_fusion.7 = f32[4608]{0:T(1024)S(1)} fusion(f32[12288]{0:T(1024)S(1)} %bitcast.139, s32[5120]{0:T(1024)S(1)} %pad_clamp_fusion), kind=kCustom, calls=%fused_computation.7 | custom fusion | bytes 55296 | tf_op jit(solution)/shard_map/gather | solution.py:74
  752.4 9.5 all-gather.6
  763.0 7.8 fusion.8
  770.8 2.3 scatter_custom_fusion.2
  773.2 3.2 broadcast_select_fusion.1
  776.4 50.5 %all-reduce.10.cloned.1.call-done = f32[36864]{0:T(1024)} async-done(((f32[36864]{0:T(1024)}), f32[36864]{0:T(1024)}) %all-reduce.10.cloned.1.call-update) | async-done | bytes 147472 | tf_op jit(solution)/shard_map/psum | solution.py:54
  826.9 1.5 multiply_reduce_fusion.3
  828.4 39.5 %psum.107 = f32[]{:T(128)} all-reduce(f32[]{:T(128)} %get-tuple-element.93), channel_id=1, replica_groups=mesh['row'=4,'col'=8] {'row','col'}, use_global_device_ids=true, to_apply=%region_23.24 | all-reduce | flops 1 | bytes 8 | tf_op jit(solution)/shard_map/psum | solution.py:79
  867.8 1.9 multiply_reduce_fusion.2
  869.8 1.3 scatter.24
  871.1 40.6 %psum.108 = f32[]{:T(128)} all-reduce(f32[]{:T(128)} %multiply_reduce_fusion.2), channel_id=1, replica_groups=mesh['row'=4,'col'=8] {'row','col'}, use_global_device_ids=true, to_apply=%region_25.26 | all-reduce | flops 1 | bytes 8 | tf_op jit(solution)/shard_map/psum | solution.py:79
  911.7 2.5 multiply_reduce_fusion.1
  914.2 40.4 %psum.109 = f32[]{:T(128)} all-reduce(f32[]{:T(128)} %get-tuple-element.91), channel_id=1, replica_groups=mesh['row'=4,'col'=8] {'row','col'}, use_global_device_ids=true, to_apply=%region_27.28 | all-reduce | flops 1 | bytes 8 | tf_op jit(solution)/shard_map/psum | solution.py:79
  955.9 40.5 %psum.110 = f32[]{:T(128)} all-reduce(f32[]{:T(128)} %multiply_reduce_fusion), channel_id=1, replica_groups=mesh['row'=4,'col'=8] {'row','col'}, use_global_device_ids=true, to_apply=%region_29.30 | all-reduce | flops 1 | bytes 8 | tf_op jit(solution)/shard_map/psum | solution.py:64
  997.1 3.9 broadcast_select_fusion
  1001.0 1.5 scatter.26
  1006.1 9.3 all-gather.7
  1016.4 7.8 fusion.6
  1024.2 2.3 scatter_custom_fusion.3
  1026.5 52.8 %all-reduce.12.cloned.1.call-done = f32[36864]{0:T(1024)} async-done(((f32[36864]{0:T(1024)}), f32[36864]{0:T(1024)}) %all-reduce.12.cloned.1.call-update) | async-done | bytes 147472 | tf_op jit(solution)/shard_map/psum | solution.py:54
  (102 shorter events, 22.3 us)
Async XLA Ops:
  7.2 244.2 %all-reduce.6.cloned.1.call-start = ((), (), s32[]{:S(2)}) async-start(), calls=%async_computation | async-start | bytes 294912 | tf_op jit(solution)/shard_map/psum | solution.py:54
  69.4 75.9 %copy-start.1 = (s32[1,1,24]{2,1,0:T(1,128)S(1)}, s32[1,1,24]{2,1,0:T(1,128)}, u32[]{:S(2)}) copy-start(s32[1,1,24]{2,1,0:T(1,128)} %param.29) | copy-start | bytes 292
  153.3 33.7 %copy-start.2 = (s32[1,1,256]{2,1,0:T(1,128)S(1)}, s32[1,1,256]{2,1,0:T(1,128)}, u32[]{:S(2)}) copy-start(s32[1,1,256]{2,1,0:T(1,128)} %param.26) | copy-start | bytes 3076
  177.4 18.9 %copy-start.3 = (f32[1,1,256]{2,1,0:T(1,128)S(1)}, f32[1,1,256]{2,1,0:T(1,128)}, u32[]{:S(2)}) copy-start(f32[1,1,256]{2,1,0:T(1,128)} %param.24) | copy-start | bytes 3076
  177.4 21.9 %copy-start = (f32[1,1,4608]{2,1,0:T(1,128)S(1)}, f32[1,1,4608]{2,1,0:T(1,128)}, u32[]{:S(2)}) copy-start(f32[1,1,4608]{2,1,0:T(1,128)} %param.22) | copy-start | bytes 55300
  177.4 22.6 %copy-start.4 = (s32[2]{0:T(128)S(1)}, s32[2]{0:T(128)}, u32[]{:S(2)}) copy-start(s32[2]{0:T(128)} %constant.236.clone.1) | copy-start | bytes 28
  198.6 318.3 %all-reduce.8.cloned.1.call-start = ((), (), s32[]{:S(2)}) async-start(), calls=%async_computation.1 | async-start | bytes 294912 | tf_op jit(solution)/shard_map/psum | solution.py:54
  464.1 362.8 %all-reduce.10.cloned.1.call-start = ((), (), s32[]{:S(2)}) async-start(), calls=%async_computation.2 | async-start | bytes 294912 | tf_op jit(solution)/shard_map/psum | solution.py:54
  773.1 306.2 %all-reduce.12.cloned.1.call-start = ((), (), s32[]{:S(2)}) async-start(), calls=%async_computation.3 | async-start | bytes 294912 | tf_op jit(solution)/shard_map/psum | solution.py:54
Sparse Core Ops, SparseCore 0:
  198.7 52.6 all-reduce.5
  464.2 52.6 all-reduce.7
  773.2 53.5 all-reduce.9
  1026.6 52.6 all-reduce.11
where the time goes:
time: 1090 us
  blocking collectives  440 us (40%)
  local copies, waits for them, and re-layouts  311 us (29%)
  waiting for transfers between devices  206 us (19%)
  other arithmetic  56.7 us (5%)
  matrix products  56.1 us (5%)
  between operations  17.6 us (2%)
    psum x6, blocking collectives, local(): height = lax.psum(jnp.sum(earlier * image), ('row', 'col'))  240 us
    gather x6, local copies, waits for them, and re-layouts, local(): low_vector[gather_spot]  228 us
    psum x4, waiting for transfers between devices, kernel_apply(): row_total = lax.psum(partial_value, 'col')  206 us
    psum x4, blocking collectives, global_norm(): return jnp.sqrt(lax.psum(jnp.sum(field * field), ('row', 'col')))  162 us
    gather x3, local copies, waits for them, and re-layouts, local(): direction = result.reshape(-1)[flat_spot]  72.2 us
    all_gather x4, blocking collectives, kernel_apply(): column = lax.all_gather(low_field, 'row', axis=0, tiled=True)  37.3 us
    dot_general x4, matrix products, kernel_apply(): jnp.einsum('tij,tj->ti', local_tiles, column_pieces, preferred_element_ty...  31.1 us
    dot_general x3, matrix products, local(): jnp.einsum('fij,fj->fi', fault_blocks, padded, preferred_element_type=jnp...  23.7 us
  transfers between devices with their start and end apart: 4, of which 4 were waited for; matrix products, arithmetic and copies ran while one was open for 1% of the time, Pallas kernels for 0%

commit v1 on v0

--- a/solution.py
+++ b/solution.py
@@ -51,7 +51,7 @@
             * tile_weight[:, None]
         )
         partial_value = jax.ops.segment_sum(products, tile_rows, num_segments=row_tiles).reshape(-1)
-        row_total = lax.psum(partial_value, "col")
+        row_total = jnp.sum(lax.all_gather(partial_value, "col"), axis=0)
         return lax.dynamic_slice_in_dim(row_total, lax.axis_index("col") * vector_len, vector_len)
 
     rhs_flat = rhs.reshape(-1)

time: 1090 us -> 972 us (0.89)
  waiting for transfers between devices: 206 us -> 80.6 us
    psum x4 -> x0, waiting for transfers between devices: 206 us -> none  [kernel_apply(): row_total = lax.psum(partial_value, 'col')]
    all_gather x0 -> x4, waiting for transfers between devices: none -> 80.6 us  [kernel_apply(): row_total = jnp.sum(lax.all_gather(partial_value, 'col'), axis=0)]
where the time goes in v1:
time: 972 us; the launch traced here: 968 us
  blocking collectives  439 us (45%)
  local copies, waits for them, and re-layouts  311 us (32%)
  waiting for transfers between devices  80.6 us (8%)
  other arithmetic  62.3 us (6%)
  matrix products  56.1 us (6%)
  between operations  17.7 us (2%)
    psum x6, blocking collectives, local(): height = lax.psum(jnp.sum(earlier * image), ('row', 'col'))  240 us
    gather x6, local copies, waits for them, and re-layouts, local(): low_vector[gather_spot]  228 us
    psum x4, blocking collectives, global_norm(): return jnp.sqrt(lax.psum(jnp.sum(field * field), ('row', 'col')))  162 us
    all_gather x4, waiting for transfers between devices, kernel_apply(): row_total = jnp.sum(lax.all_gather(partial_value, 'col'), axis=0)  80.6 us
    gather x3, local copies, waits for them, and re-layouts, local(): direction = result.reshape(-1)[flat_spot]  72.2 us
    all_gather x4, blocking collectives, kernel_apply(): column = lax.all_gather(low_field, 'row', axis=0, tiled=True)  37.5 us
    dot_general x4, matrix products, kernel_apply(): jnp.einsum('tij,tj->ti', local_tiles, column_pieces, preferred_element_ty...  31.1 us
    dot_general x3, matrix products, local(): jnp.einsum('fij,fj->fi', fault_blocks, padded, preferred_element_type=jnp...  23.7 us
  transfers between devices with their start and end apart: 4, of which 4 were waited for; matrix products, arithmetic and copies ran while one was open for 1% of the time, Pallas kernels for 0%

profile of v1, /device:TPU:8, one launch (start us, length us, event | category | flops | bytes accessed | tf_op | source)
XLA Modules:
  0.0 967.5 jit_solution(16016314623661135520)
XLA Ops:
  10.4 4.5 fusion.50
  15.8 10.6 %select_select_fusion = s32[4608]{0:T(1024)S(1)} fusion(pred[4608]{0:T(1024)(128)(4,1)S(1)} %get-tuple-element.90, pred[4608]{0:T(1024)(128)(4,1)S(1)} %get-tuple-element.89, pred[4608]{0:T(1024)(128)(4,1)S(1)} %get-tuple-element.88, pred[4608]{0:T(1024)(128)(4,1)S(1)} %get-tuple-element.87, pred[4608]{0:T(1024)(128)(4,1)S(1)} %get-tuple-element.86, ...), kind=kLoop, calls=%fused_computation.100 | loop fusion | flops 78336 | bytes 115268 | tf_op jit(solution)/shard_map/gather | solution.py:43
  27.9 40.7 %psum.70 = f32[]{:T(128)} all-reduce(f32[]{:T(128)} %multiply_reduce_fusion.9), channel_id=1, replica_groups=mesh['row'=4,'col'=8] {'row','col'}, use_global_device_ids=true, to_apply=%region_1.2 | all-reduce | flops 1 | bytes 8 | tf_op jit(solution)/shard_map/psum | solution.py:64
  69.4 75.8 %gather_fusion = bf16[12288]{0:T(1024)(128)(2,1)S(1)} fusion(bf16[4608]{0:T(1024)(128)(2,1)S(1)} %fusion.59, s32[12288]{0:T(1024)S(1)} %broadcast_clamp_fusion), kind=kCustom, calls=%fused_computation | custom fusion | bytes 98304 | tf_op jit(solution)/shard_map/gather | solution.py:72
  145.3 7.9 fusion.4
  153.3 24.1 %gather_fusion.1 = f32[4608]{0:T(1024)S(1)} fusion(f32[12288]{0:T(1024)S(1)} %bitcast.140, s32[5120]{0:T(1024)S(1)} %pad_clamp_fusion), kind=kCustom, calls=%fused_computation.1 | custom fusion | bytes 55296 | tf_op jit(solution)/shard_map/gather | solution.py:74
  177.4 9.3 all-gather.4
  188.5 7.8 fusion.12
  196.2 2.3 scatter_custom_fusion
  198.7 21.6 %all-gather.17.cloned.1.call-done = f32[8,1,36864]{2,1,0:T(1,128)} async-done(((f32[1,1,36864]{2,1,0:T(1,128)}), f32[8,1,36864]{2,1,0:T(1,128)}) %all-gather.17.cloned.1.call-update) | async-done | bytes 1179664 | tf_op jit(solution)/shard_map/all_gather | solution.py:54
  220.3 2.1 reduce_sum.137
  223.2 39.4 %psum.71 = f32[]{:T(128)} all-reduce(f32[]{:T(128)} %get-tuple-element.99), channel_id=1, replica_groups=mesh['row'=4,'col'=8] {'row','col'}, use_global_device_ids=true, to_apply=%region_7.8 | all-reduce | flops 1 | bytes 8 | tf_op jit(solution)/shard_map/psum | solution.py:79
  263.8 40.5 %psum.72 = f32[]{:T(128)} all-reduce(f32[]{:T(128)} %multiply_reduce_fusion.7), channel_id=1, replica_groups=mesh['row'=4,'col'=8] {'row','col'}, use_global_device_ids=true, to_apply=%region_9.10 | all-reduce | flops 1 | bytes 8 | tf_op jit(solution)/shard_map/psum | solution.py:64
  305.7 75.8 %gather_fusion.3 = bf16[12288]{0:T(1024)(128)(2,1)S(1)} fusion(bf16[4608]{0:T(1024)(128)(2,1)S(1)} %fusion.60, s32[12288]{0:T(1024)S(1)} %broadcast_clamp_fusion), kind=kCustom, calls=%fused_computation.3 | custom fusion | bytes 98304 | tf_op jit(solution)/shard_map/gather | solution.py:72
  381.6 7.9 fusion.2
  389.6 24.1 %gather_fusion.4 = f32[4608]{0:T(1024)S(1)} fusion(f32[12288]{0:T(1024)S(1)} %bitcast.141, s32[5120]{0:T(1024)S(1)} %pad_clamp_fusion), kind=kCustom, calls=%fused_computation.4 | custom fusion | bytes 55296 | tf_op jit(solution)/shard_map/gather | solution.py:74
  413.7 9.3 all-gather.6
  424.1 7.8 fusion.10
  431.8 2.3 scatter_custom_fusion.1
  434.2 21.6 %all-gather.19.cloned.1.call-done = f32[8,1,36864]{2,1,0:T(1,128)} async-done(((f32[1,1,36864]{2,1,0:T(1,128)}), f32[8,1,36864]{2,1,0:T(1,128)}) %all-gather.19.cloned.1.call-update) | async-done | bytes 1179664 | tf_op jit(solution)/shard_map/all_gather | solution.py:54
  455.8 2.1 reduce_sum.140
  458.7 39.4 %psum.73 = f32[]{:T(128)} all-reduce(f32[]{:T(128)} %get-tuple-element.97), channel_id=1, replica_groups=mesh['row'=4,'col'=8] {'row','col'}, use_global_device_ids=true, to_apply=%region_14.15 | all-reduce | flops 1 | bytes 8 | tf_op jit(solution)/shard_map/psum | solution.py:79
  498.2 1.9 multiply_reduce_fusion.5
  500.1 40.4 %psum.74 = f32[]{:T(128)} all-reduce(f32[]{:T(128)} %multiply_reduce_fusion.5), channel_id=1, replica_groups=mesh['row'=4,'col'=8] {'row','col'}, use_global_device_ids=true, to_apply=%region_16.17 | all-reduce | flops 1 | bytes 8 | tf_op jit(solution)/shard_map/psum | solution.py:79
  540.4 2.5 multiply_reduce_fusion.4
  543.0 40.5 %psum.75 = f32[]{:T(128)} all-reduce(f32[]{:T(128)} %get-tuple-element.95), channel_id=1, replica_groups=mesh['row'=4,'col'=8] {'row','col'}, use_global_device_ids=true, to_apply=%region_18.19 | all-reduce | flops 1 | bytes 8 | tf_op jit(solution)/shard_map/psum | solution.py:64
  584.2 75.8 %gather_fusion.6 = bf16[12288]{0:T(1024)(128)(2,1)S(1)} fusion(bf16[4608]{0:T(1024)(128)(2,1)S(1)} %fusion.58, s32[12288]{0:T(1024)S(1)} %broadcast_clamp_fusion), kind=kCustom, calls=%fused_computation.6 | custom fusion | bytes 98304 | tf_op jit(solution)/shard_map/gather | solution.py:72
  660.2 7.9 fusion
  668.1 24.1 %gather_fusion.7 = f32[4608]{0:T(1024)S(1)} fusion(f32[12288]{0:T(1024)S(1)} %bitcast.139, s32[5120]{0:T(1024)S(1)} %pad_clamp_fusion), kind=kCustom, calls=%fused_computation.7 | custom fusion | bytes 55296 | tf_op jit(solution)/shard_map/gather | solution.py:74
  692.2 9.5 all-gather.8
  702.8 7.8 fusion.8
  710.6 2.3 scatter_custom_fusion.2
  716.5 3.1 broadcast_select_fusion.1
  719.6 15.7 %all-gather.21.cloned.1.call-done = f32[8,1,36864]{2,1,0:T(1,128)} async-done(((f32[1,1,36864]{2,1,0:T(1,128)}), f32[8,1,36864]{2,1,0:T(1,128)}) %all-gather.21.cloned.1.call-update) | async-done | bytes 1179664 | tf_op jit(solution)/shard_map/all_gather | solution.py:54
  735.3 2.1 reduce_sum.144
  738.2 39.4 %psum.76 = f32[]{:T(128)} all-reduce(f32[]{:T(128)} %get-tuple-element.93), channel_id=1, replica_groups=mesh['row'=4,'col'=8] {'row','col'}, use_global_device_ids=true, to_apply=%region_23.24 | all-reduce | flops 1 | bytes 8 | tf_op jit(solution)/shard_map/psum | solution.py:79
  777.6 1.9 multiply_reduce_fusion.2
  780.8 40.4 %psum.77 = f32[]{:T(128)} all-reduce(f32[]{:T(128)} %multiply_reduce_fusion.2), channel_id=1, replica_groups=mesh['row'=4,'col'=8] {'row','col'}, use_global_device_ids=true, to_apply=%region_25.26 | all-reduce | flops 1 | bytes 8 | tf_op jit(solution)/shard_map/psum | solution.py:79
  821.3 2.6 multiply_reduce_fusion.1
  823.9 40.5 %psum.78 = f32[]{:T(128)} all-reduce(f32[]{:T(128)} %get-tuple-element.91), channel_id=1, replica_groups=mesh['row'=4,'col'=8] {'row','col'}, use_global_device_ids=true, to_apply=%region_27.28 | all-reduce | flops 1 | bytes 8 | tf_op jit(solution)/shard_map/psum | solution.py:79
  865.8 40.4 %psum.79 = f32[]{:T(128)} all-reduce(f32[]{:T(128)} %multiply_reduce_fusion), channel_id=1, replica_groups=mesh['row'=4,'col'=8] {'row','col'}, use_global_device_ids=true, to_apply=%region_29.30 | all-reduce | flops 1 | bytes 8 | tf_op jit(solution)/shard_map/psum | solution.py:64
  906.8 3.9 broadcast_select_fusion
  910.8 1.5 scatter.26
  915.8 9.5 all-gather.10
  926.4 7.8 fusion.6
  934.2 2.3 scatter_custom_fusion.3
  936.5 21.6 %all-gather.23.cloned.1.call-done = f32[8,1,36864]{2,1,0:T(1,128)} async-done(((f32[1,1,36864]{2,1,0:T(1,128)}), f32[8,1,36864]{2,1,0:T(1,128)}) %all-gather.23.cloned.1.call-update) | async-done | bytes 1179664 | tf_op jit(solution)/shard_map/all_gather | solution.py:54
  958.2 2.1 reduce_sum.149
  (106 shorter events, 25.2 us)
Async XLA Ops:
  7.2 213.2 %all-gather.17.cloned.1.call-start = ((), (), s32[]{:S(2)}) async-start(), calls=%async_computation | async-start | bytes 1327104 | tf_op jit(solution)/shard_map/all_gather | solution.py:54
  69.3 75.9 %copy-start.1 = (s32[1,1,24]{2,1,0:T(1,128)S(1)}, s32[1,1,24]{2,1,0:T(1,128)}, u32[]{:S(2)}) copy-start(s32[1,1,24]{2,1,0:T(1,128)} %param.29) | copy-start | bytes 292
  153.3 33.7 %copy-start.2 = (s32[1,1,256]{2,1,0:T(1,128)S(1)}, s32[1,1,256]{2,1,0:T(1,128)}, u32[]{:S(2)}) copy-start(s32[1,1,256]{2,1,0:T(1,128)} %param.26) | copy-start | bytes 3076
  177.4 18.9 %copy-start.3 = (f32[1,1,256]{2,1,0:T(1,128)S(1)}, f32[1,1,256]{2,1,0:T(1,128)}, u32[]{:S(2)}) copy-start(f32[1,1,256]{2,1,0:T(1,128)} %param.24) | copy-start | bytes 3076
  177.4 21.3 %copy-start = (f32[1,1,4608]{2,1,0:T(1,128)S(1)}, f32[1,1,4608]{2,1,0:T(1,128)}, u32[]{:S(2)}) copy-start(f32[1,1,4608]{2,1,0:T(1,128)} %param.22) | copy-start | bytes 55300
  198.6 257.3 %all-gather.19.cloned.1.call-start = ((), (), s32[]{:S(2)}) async-start(), calls=%async_computation.1 | async-start | bytes 1327104 | tf_op jit(solution)/shard_map/all_gather | solution.py:54
  434.2 301.1 %all-gather.21.cloned.1.call-start = ((), (), s32[]{:S(2)}) async-start(), calls=%async_computation.2 | async-start | bytes 1327104 | tf_op jit(solution)/shard_map/all_gather | solution.py:54
  692.2 22.8 %copy-start.4 = (s32[2]{0:T(128)S(1)}, s32[2]{0:T(128)}, u32[]{:S(2)}) copy-start(s32[2]{0:T(128)} %constant.236.clone.1) | copy-start | bytes 28
  712.9 245.2 %all-gather.23.cloned.1.call-start = ((), (), s32[]{:S(2)}) async-start(), calls=%async_computation.3 | async-start | bytes 1327104 | tf_op jit(solution)/shard_map/all_gather | solution.py:54
Sparse Core Ops, SparseCore 0:
  198.7 21.5 all-gather.16
  434.3 21.4 all-gather.18
  713.1 22.1 all-gather.20
  936.6 21.4 all-gather.22
